TPU v7x, 128 devices: a whole 4x4x4 slice. The times are simulated.
128 devices in a mesh: req: 16 (over x_hi, y, core), tensor: 8 (over x_lo, z).
Axes of the slice: x: 4 (x_hi: 2, x_lo: 2; x = x_hi * 2 + x_lo), y: 4, z: 4, core: 2. Of those that a mesh axis runs over, the one named last changes fastest.
Arguments:
- hidden: bfloat16 [32, 512, 1792], P('req', 'tensor')
- suffix_len: int32 [32], P('req'), may hold values from 1 to 512, as said below
- request_group: int32 [32], P('req'), may hold values from 0 to 63
- group_slot: int32 [64], replicated, may hold values from 0 to 63, each once
- norm_first: float32 [1792], replicated, may hold values from 0.5 to 2
- query_weight: bfloat16 [1792, 256], P(None, 'tensor'), may hold values from -0.125 to 0.125
- key_weight: bfloat16 [1792, 256], P(None, 'tensor'), may hold values from -0.125 to 0.125
- value_weight: bfloat16 [1792, 1792], P(None, 'tensor'), may hold values from -0.125 to 0.125
- filter_gate: bfloat16 [1792, 1792], P(None, 'tensor'), may hold values from -0.125 to 0.125
- filter_taps: float32 [3, 1792], P(None, 'tensor'), may hold values from -3 to 3
- linear_out: bfloat16 [1792, 1792], P('tensor'), may hold values from -0.125 to 0.125
- norm_second: float32 [1792], replicated, may hold values from 0.5 to 1.5
- window_query: bfloat16 [1792, 1792], P(None, 'tensor')
- window_key: bfloat16 [1792, 1792], P(None, 'tensor')
- window_value: bfloat16 [1792, 1792], P(None, 'tensor'), may hold values from -0.125 to 0.125
- window_out: bfloat16 [1792, 1792], P('tensor'), may hold values from -0.125 to 0.125
- norm_third: float32 [1792], replicated, may hold values from 0.5 to 1.5
- gate_weight: bfloat16 [1792, 7168], P(None, 'tensor'), may hold values from -0.125 to 0.125
- up_weight: bfloat16 [1792, 7168], P(None, 'tensor'), may hold values from -0.125 to 0.125
- down_weight: bfloat16 [7168, 1792], P('tensor'), may hold values from -0.0625 to 0.0625
- prefix_sums: float32 [64, 16, 273, 112], P('req', 'tensor'), as said below
- prefix_norms: float32 [64, 16, 273], P('req', 'tensor'), as said below
- prefix_keys: bfloat16 [64, 64, 1792], P('req', None, 'tensor'), may hold values from -6 to 6
- prefix_values: bfloat16 [64, 64, 1792], P('req', None, 'tensor'), may hold values from -6 to 6
- prefix_tail: bfloat16 [64, 2, 1792], P('req', None, 'tensor'), may hold values from -10 to 10
Outputs:
- hidden_out: bfloat16 [32, 512, 1792], P('req', 'tensor')
- final_norm: float32 [32], P('req')
- top_logit: float32 [32], P('req')
Inputs may be any that keep to these rules, and one draw needn't show every extreme that they name: `suffix_len`: each request's suffix is either a short one of at most 32 tokens or a long one of more than 384; some request has exactly 512. `group_slot`: each slot holds exactly one group. `prefix_sums`: A sum over 128 prefix tokens of the key feature map times the value. `prefix_norms`: A sum over the same 128 tokens of the key feature map, so its inner product with any feature map is positive.
All inputs are finite; a program needn't handle non-finite values.
Results may differ from a plain program's by a relative error of at most 0.024.
Values may be sent and summed in bfloat16 or wider, within the bound.
A program may use at most 128 MiB of HBM per device.

v0:
```python
import jax
import jax.numpy as jnp
from jax import lax
from jax.sharding import PartitionSpec as P

D = 1792
FD = 16
HS = 112
WIN = 64
KC = 3
LMAX = 512
EPS = 1e-05


def rms_norm(row_block, gain_vector):
    floats = row_block.astype(jnp.float32)
    inverse_rms = lax.rsqrt(jnp.mean(floats * floats, axis=-1, keepdims=True) + EPS)
    return (floats * inverse_rms * gain_vector).astype(jnp.bfloat16)


def features(vectors):
    floats = vectors.astype(jnp.float32)
    dimension = floats.shape[-1]
    constant = jnp.ones(floats.shape[:-1] + (1,), jnp.float32)
    linear_part = floats * dimension ** (-0.25)
    square_part = (floats[..., :, None] * floats[..., None, :]).reshape(
        floats.shape[:-1] + (dimension * dimension,)
    )
    square_part = square_part * (2.0 * dimension) ** (-0.5)
    return jnp.concatenate([constant, linear_part, square_part], axis=-1)


def slot_lookup(groups, group_slot):
    matches = jnp.arange(group_slot.shape[0])[None, :] == groups[:, None]
    return jnp.sum(jnp.where(matches, group_slot[None, :], 0), axis=1)


def per_device(
    hidden,
    suffix_len,
    request_group,
    group_slot,
    norm_first,
    query_weight,
    key_weight,
    value_weight,
    filter_gate,
    filter_taps,
    linear_out,
    norm_second,
    window_query,
    window_key,
    window_value,
    window_out,
    norm_third,
    gate_weight,
    up_weight,
    down_weight,
    prefix_sums,
    prefix_norms,
    prefix_keys,
    prefix_values,
    prefix_tail,
):
    requests_here = hidden.shape[0]
    share_rows = hidden.shape[1]
    model_width = hidden.shape[2]
    lin_heads = prefix_sums.shape[1]
    win_heads = prefix_keys.shape[2] // HS
    slot_ids = slot_lookup(request_group, group_slot)
    all_sums, all_norms = (
        lax.all_gather(prefix_sums.astype(jnp.bfloat16), "req", axis=0, tiled=True).astype(
            prefix_sums.dtype
        ),
        lax.all_gather(prefix_norms.astype(jnp.bfloat16), "req", axis=0, tiled=True).astype(
            prefix_norms.dtype
        ),
    )
    all_keys, all_values, all_tails = (
        lax.all_gather(prefix_keys, "req", axis=0, tiled=True),
        lax.all_gather(prefix_values, "req", axis=0, tiled=True),
        lax.all_gather(prefix_tail, "req", axis=0, tiled=True),
    )
    picked_sum = jnp.take(all_sums, slot_ids, axis=0)
    picked_norm = jnp.take(all_norms, slot_ids, axis=0)
    picked_keys = jnp.take(all_keys, slot_ids, axis=0)
    picked_values = jnp.take(all_values, slot_ids, axis=0)
    picked_tail = jnp.take(all_tails, slot_ids, axis=0)

    def settle(stream, partial_sum, gain_vector):
        summed = lax.psum(partial_sum.astype(jnp.bfloat16), "tensor").astype(jnp.float32)
        stream = (stream.astype(jnp.float32) + summed).astype(jnp.bfloat16)
        normed = None if gain_vector is None else rms_norm(stream, gain_vector)
        return (stream, normed)

    stream = lax.all_gather(hidden, "tensor", axis=1, tiled=True)
    normed = rms_norm(stream, norm_first)
    position = jnp.arange(LMAX)
    causal = position[:, None] >= position[None, :]
    key_place = jnp.arange(WIN + LMAX)
    allowed = (key_place[None, :] > position[:, None]) & (
        key_place[None, :] <= position[:, None] + WIN
    )

    def project(normed_rows, matrix):
        flat_rows = normed_rows.reshape(requests_here * LMAX, model_width)
        return jnp.dot(flat_rows, matrix, preferred_element_type=jnp.float32).astype(jnp.bfloat16)

    queries = project(normed, query_weight).reshape(requests_here, LMAX, lin_heads, FD)
    key_rows = project(normed, key_weight).reshape(requests_here, LMAX, lin_heads, FD)
    values_lin = project(normed, value_weight).reshape(requests_here, LMAX, lin_heads * HS)
    gating = project(normed, filter_gate).reshape(requests_here, LMAX, lin_heads * HS)
    extended = jnp.concatenate([picked_tail, values_lin], axis=1).astype(jnp.float32)
    convolved = sum(
        (
            filter_taps[offset] * extended[:, KC - 1 - offset : KC - 1 - offset + LMAX]
            for offset in range(KC)
        )
    )
    mixed_values = (
        (convolved * jax.nn.silu(gating.astype(jnp.float32)))
        .astype(jnp.bfloat16)
        .reshape(requests_here, LMAX, lin_heads, HS)
    )
    scores = jnp.einsum(
        "rthf,rshf->rhts", queries, key_rows, preferred_element_type=jnp.float32
    ) * FD ** (-0.5)
    weights_lin = jnp.where(causal, 1.0 + scores + 0.5 * scores * scores, 0.0)
    numerator = jnp.einsum(
        "rhts,rshd->rthd",
        weights_lin.astype(jnp.bfloat16),
        mixed_values,
        preferred_element_type=jnp.float32,
    )
    denominator = jnp.transpose(jnp.sum(weights_lin, axis=-1), (0, 2, 1))
    mapped = features(queries)
    numerator = numerator + jnp.einsum(
        "rthf,rhfd->rthd", mapped, picked_sum, precision=lax.Precision.HIGHEST
    )
    denominator = denominator + jnp.einsum(
        "rthf,rhf->rth", mapped, picked_norm, precision=lax.Precision.HIGHEST
    )
    linear_rows = (
        (numerator / denominator[..., None])
        .astype(jnp.bfloat16)
        .reshape(requests_here * LMAX, lin_heads * HS)
    )
    partial_sum = jnp.dot(linear_rows, linear_out, preferred_element_type=jnp.float32).reshape(
        requests_here, LMAX, model_width
    )
    stream, normed = settle(stream, partial_sum, norm_second)
    window_q = project(normed, window_query).reshape(requests_here, LMAX, win_heads, HS)
    window_k = project(normed, window_key).reshape(requests_here, LMAX, win_heads * HS)
    window_v = project(normed, window_value).reshape(requests_here, LMAX, win_heads * HS)
    all_keys = jnp.concatenate([picked_keys, window_k], axis=1).reshape(
        requests_here, WIN + LMAX, win_heads, HS
    )
    all_values = jnp.concatenate([picked_values, window_v], axis=1).reshape(
        requests_here, WIN + LMAX, win_heads, HS
    )
    logits = jnp.einsum(
        "rthd,rphd->rhtp", window_q, all_keys, preferred_element_type=jnp.float32
    ) * HS ** (-0.5)
    logits = jnp.where(allowed, logits, -jnp.inf)
    row_max = jnp.max(logits, axis=-1, keepdims=True)
    exponent = jnp.exp(logits - row_max)
    probabilities = (exponent / jnp.sum(exponent, axis=-1, keepdims=True)).astype(jnp.bfloat16)
    attended = jnp.einsum(
        "rhtp,rphd->rthd", probabilities, all_values, preferred_element_type=jnp.float32
    ).astype(jnp.bfloat16)
    attended = attended.reshape(requests_here * LMAX, win_heads * HS)
    final_whole = position[None, :] == suffix_len[:, None] - 1
    local_top = jnp.max(jnp.where(final_whole[:, None, :], row_max[..., 0], -jnp.inf), axis=(1, 2))
    partial_sum = jnp.dot(attended, window_out, preferred_element_type=jnp.float32).reshape(
        requests_here, LMAX, model_width
    )
    stream, normed = settle(stream, partial_sum, norm_third)
    flat_rows = normed.reshape(requests_here * LMAX, model_width)
    gate_rows = jnp.dot(flat_rows, gate_weight, preferred_element_type=jnp.float32)
    up_rows = jnp.dot(flat_rows, up_weight, preferred_element_type=jnp.float32)
    inner_rows = (jax.nn.silu(gate_rows) * up_rows).astype(jnp.bfloat16)
    partial_sum = jnp.dot(inner_rows, down_weight, preferred_element_type=jnp.float32).reshape(
        requests_here, LMAX, model_width
    )
    stream, unused = settle(stream, partial_sum, None)
    row_start = lax.axis_index("tensor") * share_rows
    stream = lax.dynamic_slice_in_dim(stream, row_start, share_rows, 1)
    rows_here = row_start + jnp.arange(share_rows)
    valid = rows_here[None, :] < suffix_len[:, None]
    hidden_out = jnp.where(valid[..., None], stream, jnp.zeros_like(stream))
    stream_f = stream.astype(jnp.float32)
    live_term = jnp.sum(jnp.where(valid[..., None], stream_f * stream_f, 0.0), axis=(1, 2))
    squares = lax.psum(live_term, "tensor")
    top_logit = lax.pmax(local_top, "tensor")
    return (hidden_out, jnp.sqrt(squares / D), top_logit)


def solution(mesh):
    return jax.shard_map(
        per_device,
        mesh=mesh,
        in_specs=(
            P("req", "tensor", None),
            P("req"),
            P("req"),
            P(),
            P(),
            P(None, "tensor"),
            P(None, "tensor"),
            P(None, "tensor"),
            P(None, "tensor"),
            P(None, "tensor"),
            P("tensor", None),
            P(),
            P(None, "tensor"),
            P(None, "tensor"),
            P(None, "tensor"),
            P("tensor", None),
            P(),
            P(None, "tensor"),
            P(None, "tensor"),
            P("tensor", None),
            P("req", "tensor", None, None),
            P("req", "tensor", None),
            P("req", None, "tensor"),
            P("req", None, "tensor"),
            P("req", None, "tensor"),
        ),
        out_specs=(P("req", "tensor", None), P("req"), P("req")),
        check_vma=False,
    )
```

profile of v0, /device:TPU:0, one launch (start us, length us, event | category | flops | bytes accessed | tf_op | source)
XLA Modules:
  0.0 618.0 jit_solution(13063100441761800405)
XLA Ops:
  7.2 0.7 all-gather.5.cloned.1.call-update
  8.0 2.6 convert_element_type.139
  10.7 0.7 all-gather.9.cloned.1.call-update
  12.0 0.9 fusion.52
  13.3 0.8 iota_compare_fusion.2
  14.1 0.7 convert_element_type.142
  14.8 25.2 %all_gather.21 = bf16[64,2,273]{2,1,0:T(2,128)(2,1)S(1)} all-gather(bf16[4,2,273]{2,1,0:T(2,128)(2,1)S(1)} %convert_element_type.142), channel_id=1, replica_groups=mesh['req'=16,'tensor'=8] {'req'}, dimensions={0}, use_global_device_ids=true | all-gather | bytes 74256 | tf_op jit(solution)/shard_map/all_gather | solution.py:75
  40.1 20.3 %all_gather.19 = bf16[64,2,224]{2,1,0:T(2,128)(2,1)S(1)} all-gather(bf16[4,2,224]{2,1,0:T(2,128)(2,1)} %param.51), channel_id=1, replica_groups=mesh['req'=16,'tensor'=8] {'req'}, dimensions={0}, use_global_device_ids=true | all-gather | bytes 60928 | tf_op jit(solution)/shard_map/all_gather | solution.py:82
  61.9 0.6 fusion.67
  62.6 3.0 fusion
  65.7 0.9 fusion.2
  66.6 1.8 copy-done.1
  68.4 1.2 convolution_convert_fusion.9
  69.6 3.9 convolution_convert_fusion.8
  73.6 1.5 reshape.191
  75.0 3.5 convolution_convert_fusion.7
  79.2 1.3 copy-done.7
  80.4 1.5 fusion.17
  82.0 1.4 fusion.11
  84.2 1.2 fusion.24
  85.5 0.7 fusion.29
  86.2 2.1 fusion.14
  88.3 48.6 %all-gather.7.cloned.1.call-done = bf16[64,2,273,112]{3,1,2,0:T(2,128)(2,1)} async-done(((bf16[4,2,273,112]{3,1,2,0:T(2,128)(2,1)}), bf16[64,2,273,112]{3,1,2,0:T(2,128)(2,1)}) %all-gather.7.cloned.1.call-update) | async-done | bytes 7827472 | tf_op jit(solution)/shard_map/all_gather | solution.py:72
  137.0 9.5 %convert_element_type.140 = f32[64,2,273,112]{3,1,2,0:T(2,128)} convert(bf16[64,2,273,112]{3,1,2,0:T(2,128)(2,1)} %all-gather.7.cloned.1.call-done) | non-fusion elementwise | flops 3913728 | bytes 23482368 | tf_op jit(solution)/shard_map/convert_element_type | solution.py:72
  146.5 8.2 %gather_fusion.1 = f32[2,2,273,112]{3,1,2,0:T(2,128)} fusion(f32[64,2,273,112]{3,1,2,0:T(2,128)} %convert_element_type.140, s32[1024]{0:T(1024)} %copy-done.19), kind=kCustom, calls=%fused_computation.3 | custom fusion | bytes 978440 | tf_op jit(solution)/shard_map/jit(_take)/gather | solution.py:84
  154.7 1.4 broadcast_select_fusion
  156.1 4.0 fusion.23
  160.2 3.0 convolution_convert_fusion.2
  163.5 21.2 %all-gather.9.cloned.1.call-done = bf16[64,64,224]{2,1,0:T(8,128)(2,1)} async-done(((bf16[4,64,224]{2,1,0:T(8,128)(2,1)}), bf16[64,64,224]{2,1,0:T(8,128)(2,1)}) %all-gather.9.cloned.1.call-update) | async-done | bytes 1835024 | tf_op jit(solution)/shard_map/all_gather | solution.py:81
  184.7 2.8 gather_fusion.3
  187.5 45.8 %all-gather.11.cloned.1.call-done = bf16[64,64,224]{2,1,0:T(8,128)(2,1)} async-done(((bf16[4,64,224]{2,1,0:T(8,128)(2,1)}), bf16[64,64,224]{2,1,0:T(8,128)(2,1)}) %all-gather.11.cloned.1.call-update) | async-done | bytes 1835024 | tf_op jit(solution)/shard_map/all_gather | solution.py:80
  233.3 2.8 gather_fusion.4
  236.1 1.6 broadcast_select_fusion.3
  237.7 1.6 copy.87
  239.3 1.6 copy.85
  240.8 90.9 %all-reduce.4.cloned.1.call-done = bf16[2,512,1792]{2,1,0:T(8,128)(2,1)} async-done(((bf16[2,512,1792]{2,1,0:T(8,128)(2,1)}), bf16[2,512,1792]{2,1,0:T(8,128)(2,1)}) %all-reduce.4.cloned.1.call-update) | async-done | bytes 3670032 | tf_op jit(solution)/shard_map/psum | solution.py:91
  331.7 4.5 fusion.4
  336.3 0.9 fusion.6
  337.2 0.9 copy-done.3
  338.1 1.8 copy-done.8
  339.9 2.0 convolution_convert_fusion.3
  341.9 2.1 concatenate.28
  344.1 1.8 copy.88
  345.9 4.3 convolution_convert_fusion.4
  350.2 2.1 reshape.193
  352.3 4.3 convolution_convert_fusion.5
  356.6 2.1 concatenate.25
  358.7 1.1 copy.86
  359.8 2.5 fusion.8
  362.3 1.0 fusion.10
  363.3 1.7 fusion.22
  365.0 3.0 convolution_convert_fusion.1
  368.3 96.2 %all-reduce.6.cloned.1.call-done = bf16[2,512,1792]{2,1,0:T(8,128)(2,1)} async-done(((bf16[2,512,1792]{2,1,0:T(8,128)(2,1)}), bf16[2,512,1792]{2,1,0:T(8,128)(2,1)}) %all-reduce.6.cloned.1.call-update) | async-done | bytes 3670032 | tf_op jit(solution)/shard_map/psum | solution.py:91
  464.5 7.4 %fusion.9 = (f32[2,512,1792]{2,1,0:T(8,128)}, f32[2,512]{1,0:T(2,128)S(1)}) fusion(bf16[2,512,1792]{2,1,0:T(8,128)(2,1)} %all-reduce.6.cloned.1.call-done, bf16[2,512,1792]{2,1,0:T(8,128)(2,1)} %copy-done.3), kind=kLoop, calls=%fused_computation.29 | loop fusion | flops 12844032 | bytes 14684160 | tf_op jit(solution)/shard_map/convert_element_type | solution.py:92
  472.0 1.3 multiply_convert_fusion
  473.3 1.8 copy-done.9
  475.1 5.9 fusion.68
  481.0 12.5 %convolution_convert_fusion = bf16[1024,1792]{1,0:T(8,128)(2,1)} fusion(bf16[896,1792]{1,0:T(8,128)(2,1)S(1)} %copy-done, f32[1024,896]{1,0:T(8,128)} %fusion.68, bf16[1024,1792]{1,0:T(8,128)(2,1)} %bitcast.103, bf16[1792,896]{1,0:T(8,128)(2,1)} %param.45), kind=kOutput, calls=%fused_computation.26 | convolution fusion | flops 6584008704 | bytes 17432576 | tf_op jit(solution)/shard_map/dot_general | solution.py:182
  493.5 0.6 copy-done.27
  494.4 18.8 %pmax.7 = f32[2]{0:T(128)} all-reduce(f32[2]{0:T(128)S(1)} %select_reduce_fusion.1), channel_id=1, replica_groups=mesh['req'=16,'tensor'=8] {'tensor'}, use_global_device_ids=true, to_apply=%region_13.15 | all-reduce | flops 2 | bytes 16 | tf_op jit(solution)/shard_map/pmax | solution.py:194
  513.1 77.0 %all-reduce.8.cloned.1.call-done = bf16[2,512,1792]{2,1,0:T(8,128)(2,1)} async-done(((bf16[2,512,1792]{2,1,0:T(8,128)(2,1)}), bf16[2,512,1792]{2,1,0:T(8,128)(2,1)}) %all-reduce.8.cloned.1.call-update) | async-done | bytes 3670032 | tf_op jit(solution)/shard_map/psum | solution.py:91
  590.1 1.6 select_reduce_fusion
  591.8 0.9 broadcast_select_fusion.1
  592.7 17.9 %psum.31 = f32[2]{0:T(128)S(1)} all-reduce(f32[2]{0:T(128)S(1)} %get-tuple-element.4), channel_id=1, replica_groups=mesh['req'=16,'tensor'=8] {'tensor'}, use_global_device_ids=true, to_apply=%region_11.13 | all-reduce | flops 2 | bytes 16 | tf_op jit(solution)/shard_map/psum | solution.py:193
  (97 shorter events, 5.8 us)
Async XLA Ops:
  7.2 473.8 %copy-start = (bf16[896,1792]{1,0:T(8,128)(2,1)S(1)}, bf16[896,1792]{1,0:T(8,128)(2,1)}, u32[]{:S(2)}) copy-start(bf16[896,1792]{1,0:T(8,128)(2,1)} %param.46) | copy-start | bytes 9633796
  7.2 54.8 %copy-start.23 = (f32[3,224]{1,0:T(4,128)S(1)}, f32[3,224]{1,0:T(4,128)}, u32[]{:S(2)}) copy-start(f32[3,224]{1,0:T(4,128)} %param.36) | copy-start | bytes 8068
  7.2 58.4 %copy-start.16 = (f32[1792]{0:T(1024)S(1)}, f32[1792]{0:T(1024)}, u32[]{:S(2)}) copy-start(f32[1792]{0:T(1024)} %param.31) | copy-start | bytes 21508
  7.2 55.4 %all-gather.5.cloned.1.call-start = ((), (), s32[]{:S(2)}) async-start(), calls=%async_computation | async-start | bytes 4128768 | tf_op jit(solution)/shard_map/all_gather | solution.py:96
  7.9 129.0 %all-gather.7.cloned.1.call-start = ((), (), s32[]{:S(2)}) async-start(), calls=%async_computation.1 | async-start | bytes 9504768 | tf_op jit(solution)/shard_map/all_gather | solution.py:72
  10.6 174.1 %all-gather.9.cloned.1.call-start = ((), (), s32[]{:S(2)}) async-start(), calls=%async_computation.3 | async-start | bytes 2228224 | tf_op jit(solution)/shard_map/all_gather | solution.py:81
  11.4 222.0 %all-gather.11.cloned.1.call-start = ((), (), s32[]{:S(2)}) async-start(), calls=%async_computation.4 | async-start | bytes 2228224 | tf_op jit(solution)/shard_map/all_gather | solution.py:80
  11.9 319.8 %all-reduce.4.cloned.1.call-start = ((), (), s32[]{:S(2)}) async-start(), calls=%async_computation.2 | async-start | bytes 7340032 | tf_op jit(solution)/shard_map/psum | solution.py:91
  12.8 0.5 copy-start.28
  14.1 46.9 %copy-start.19 = (s32[1024]{0:T(1024)}, s32[1024]{0:T(1024)S(1)}, u32[]{:S(2)}) copy-start(s32[1024]{0:T(1024)S(1)} %pad_clamp_fusion.1) | copy-start | bytes 12292
  62.6 3.1 copy-start.5
  65.7 2.7 copy-start.14
  66.6 1.8 copy-start.1
  78.5 3.5 copy-start.12
  78.5 3.4 copy-start.15
  79.2 1.3 copy-start.7
  82.0 2.1 copy-start.2
  82.0 2.3 copy-start.25
  83.4 2.0 copy-start.20
  83.4 2.0 copy-start.21
  83.5 2.0 copy-start.22
  154.7 5.5 copy-start.10
  160.2 3.1 copy-start.29
  163.3 301.3 %all-reduce.6.cloned.1.call-start = ((), (), s32[]{:S(2)}) async-start(), calls=%async_computation.5 | async-start | bytes 7340032 | tf_op jit(solution)/shard_map/psum | solution.py:91
  240.8 95.4 %copy-start.17 = (f32[1792]{0:T(1024)S(1)}, f32[1792]{0:T(1024)}, u32[]{:S(2)}) copy-start(f32[1792]{0:T(1024)} %param.38) | copy-start | bytes 21508
  336.2 1.9 copy-start.3
  336.3 3.7 copy-start.26
  338.1 1.8 copy-start.8
  362.3 1.0 copy-start.13
  363.3 1.7 copy-start.11
  368.0 103.9 %copy-start.18 = (f32[1792]{0:T(1024)S(1)}, f32[1792]{0:T(1024)}, u32[]{:S(2)}) copy-start(f32[1792]{0:T(1024)} %param.43) | copy-start | bytes 21508
  368.0 222.1 %all-reduce.8.cloned.1.call-start = ((), (), s32[]{:S(2)}) async-start(), calls=%async_computation.6 | async-start | bytes 7340032 | tf_op jit(solution)/shard_map/psum | solution.py:91
  464.5 7.4 %copy-start.4 = (bf16[2,512,1792]{2,1,0:T(8,128)(2,1)S(1)}, bf16[2,512,1792]{2,1,0:T(8,128)(2,1)}, u32[]{:S(2)}) copy-start(bf16[2,512,1792]{2,1,0:T(8,128)(2,1)} %copy-done.3) | copy-start | bytes 11010052
  464.5 7.4 %copy-start.6 = (bf16[2,512,1792]{2,1,0:T(8,128)(2,1)S(1)}, bf16[2,512,1792]{2,1,0:T(8,128)(2,1)}, u32[]{:S(2)}) copy-start(bf16[2,512,1792]{2,1,0:T(8,128)(2,1)} %all-reduce.6.cloned.1.call-done) | copy-start | bytes 11010052
  472.0 3.2 copy-start.24
  473.3 1.8 copy-start.9
  493.5 0.7 copy-start.27
Sparse Core Ops, SparseCore 0:
  9.7 50.9 all-gather.4
  63.0 73.8 all-gather.6
  139.4 45.2 all-gather.8
  187.0 46.2 all-gather.10
  235.7 95.9 all-reduce.3
  368.1 96.3 all-reduce.5
  493.6 96.4 all-reduce.7
where the time goes:
time: 619 us; the launch traced here: 618 us
  waiting for transfers between devices  382 us (62%)
  blocking collectives  82.2 us (13%)
  matrix products  57.9 us (9%)
  other arithmetic  41.5 us (7%)
  local copies, waits for them, and re-layouts  39.4 us (6%)
  between operations  14.6 us (2%)
    psum x3, waiting for transfers between devices, settle(): lax.psum(partial_sum.astype(jnp.bfloat16), 'tensor').astype(jnp.float32)  264 us
    all_gather x1, waiting for transfers between devices, per_device(): lax.all_gather(prefix_sums.astype(jnp.bfloat16), 'req', axis=0, tiled=True)  48.6 us
    all_gather x1, waiting for transfers between devices, per_device(): lax.all_gather(prefix_keys, 'req', axis=0, tiled=True)  45.8 us
    all_gather x1, blocking collectives, per_device(): lax.all_gather(prefix_norms.astype(jnp.bfloat16), 'req', axis=0, tiled=True)  25.2 us
    all_gather x1, waiting for transfers between devices, per_device(): lax.all_gather(prefix_values, 'req', axis=0, tiled=True)  21.2 us
    all_gather x1, blocking collectives, per_device(): lax.all_gather(prefix_tail, 'req', axis=0, tiled=True)  20.3 us
    dot_general x7, matrix products, project(): jnp.dot(flat_rows, matrix, preferred_element_type=jnp.float32)  20.3 us
    pmax x1, blocking collectives, per_device(): top_logit = lax.pmax(local_top, 'tensor')  18.8 us
  transfers between devices with their start and end apart: 7, of which 6 were waited for; matrix products, arithmetic and copies ran while one was open for 11% of the time, Pallas kernels for 0%

commit v1 on v0

--- a/solution.py
+++ b/solution.py
@@ -88,7 +88,9 @@
     picked_tail = jnp.take(all_tails, slot_ids, axis=0)
 
     def settle(stream, partial_sum, gain_vector):
-        summed = lax.psum(partial_sum.astype(jnp.bfloat16), "tensor").astype(jnp.float32)
+        summed = jnp.sum(lax.all_gather(partial_sum.astype(jnp.bfloat16), "tensor"), axis=0).astype(
+            jnp.float32
+        )
         stream = (stream.astype(jnp.float32) + summed).astype(jnp.bfloat16)
         normed = None if gain_vector is None else rms_norm(stream, gain_vector)
         return (stream, normed)

time: 619 us -> 1240 us (2.00)
  waiting for transfers between devices: 382 us -> 945 us
  other arithmetic: 41.5 us -> 94.2 us
    all_gather x0 -> x3, waiting for transfers between devices: none -> 838 us  [settle(): lax.all_gather(partial_sum.astype(jnp.bfloat16), 'tensor')]
    psum x3 -> x0, waiting for transfers between devices: 264 us -> none  [settle(): lax.psum(partial_sum.astype(jnp.bfloat16), 'tensor').astype(jnp.float32)]
    reduce_sum x0 -> x3, other arithmetic: none -> 38.8 us  [settle(): jnp.sum(lax.all_gather(partial_sum.astype(jnp.bfloat16), 'tensor'), axis=0)]
    all_gather x1, waiting for transfers between devices: 45.8 us -> 9.35 us  [per_device(): lax.all_gather(prefix_keys, 'req', axis=0, tiled=True)]
    all_gather x1, waiting for transfers between devices: 21.2 us -> 45.8 us  [per_device(): lax.all_gather(prefix_values, 'req', axis=0, tiled=True)]
  transfers between devices with their start and end apart: 7 -> 7, of which waited for: 6 -> 6; matrix products, arithmetic and copies ran while one was open for 11% -> 6% of each run, Pallas kernels for 0% -> 0%
where the time goes in v1:
time: 1240 us; the launch traced here: 1230 us
  waiting for transfers between devices  945 us (76%)
  other arithmetic  94.2 us (8%)
  blocking collectives  79.9 us (6%)
  matrix products  55 us (4%)
  local copies, waits for them, and re-layouts  39.6 us (3%)
  between operations  15 us (1%)
    all_gather x3, waiting for transfers between devices, settle(): lax.all_gather(partial_sum.astype(jnp.bfloat16), 'tensor')  838 us
    all_gather x1, waiting for transfers between devices, per_device(): lax.all_gather(prefix_sums.astype(jnp.bfloat16), 'req', axis=0, tiled=True)  49.6 us
    all_gather x1, waiting for transfers between devices, per_device(): lax.all_gather(prefix_values, 'req', axis=0, tiled=True)  45.8 us
    reduce_sum x3, other arithmetic, settle(): jnp.sum(lax.all_gather(partial_sum.astype(jnp.bfloat16), 'tensor'), axis=0)  38.8 us
    all_gather x1, blocking collectives, per_device(): lax.all_gather(prefix_tail, 'req', axis=0, tiled=True)  25.2 us
  transfers between devices with their start and end apart: 7, of which 6 were waited for; matrix products, arithmetic and copies ran while one was open for 6% of the time, Pallas kernels for 0%

profile of v1, /device:TPU:0, one launch (start us, length us, event | category | flops | bytes accessed | tf_op | source)
XLA Modules:
  0.0 1228.7 jit_solution(9914443987479524082)
XLA Ops:
  7.2 0.7 all-gather.10.cloned.1.call-update
  8.0 2.7 convert_element_type.152
  12.0 0.9 fusion.52
  12.9 0.8 iota_compare_fusion.2
  13.7 1.3 fusion.67
  15.0 0.7 convert_element_type.155
  15.7 25.2 %all_gather.35 = bf16[64,2,224]{2,1,0:T(2,128)(2,1)S(1)} all-gather(bf16[4,2,224]{2,1,0:T(2,128)(2,1)} %param.51), channel_id=1, replica_groups=mesh['req'=16,'tensor'=8] {'req'}, dimensions={0}, use_global_device_ids=true | all-gather | bytes 60928 | tf_op jit(solution)/shard_map/all_gather | solution.py:82
  40.9 20.4 %all_gather.37 = bf16[64,2,273]{2,1,0:T(2,128)(2,1)S(1)} all-gather(bf16[4,2,273]{2,1,0:T(2,128)(2,1)S(1)} %convert_element_type.155), channel_id=1, replica_groups=mesh['req'=16,'tensor'=8] {'req'}, dimensions={0}, use_global_device_ids=true | all-gather | bytes 74256 | tf_op jit(solution)/shard_map/all_gather | solution.py:75
  63.0 3.0 fusion
  66.1 0.9 fusion.2
  67.0 1.8 copy-done.1
  68.8 1.2 convolution_convert_fusion.8
  70.7 3.5 convolution_convert_fusion.9
  74.2 3.5 convolution_convert_fusion.7
  78.3 1.3 copy-done.7
  79.6 1.5 fusion.17
  81.2 1.4 fusion.11
  83.4 1.2 fusion.24
  84.7 0.7 fusion.29
  85.4 2.1 fusion.14
  87.5 49.6 %all-gather.12.cloned.1.call-done = bf16[64,2,273,112]{3,1,2,0:T(2,128)(2,1)} async-done(((bf16[4,2,273,112]{3,1,2,0:T(2,128)(2,1)}), bf16[64,2,273,112]{3,1,2,0:T(2,128)(2,1)}) %all-gather.12.cloned.1.call-update) | async-done | bytes 7827472 | tf_op jit(solution)/shard_map/all_gather | solution.py:72
  137.1 21.5 %convert_element_type.153 = f32[64,2,273,112]{3,1,2,0:T(2,128)} convert(bf16[64,2,273,112]{3,1,2,0:T(2,128)(2,1)} %all-gather.12.cloned.1.call-done) | non-fusion elementwise | flops 3913728 | bytes 23482368 | tf_op jit(solution)/shard_map/convert_element_type | solution.py:72
  158.6 8.0 gather_fusion.1
  166.6 1.5 broadcast_select_fusion
  168.1 4.0 fusion.23
  172.2 3.0 convolution_convert_fusion.2
  175.5 9.4 all-gather.16.cloned.1.call-done
  184.8 2.8 gather_fusion.4
  187.6 45.8 %all-gather.14.cloned.1.call-done = bf16[64,64,224]{2,1,0:T(8,128)(2,1)} async-done(((bf16[4,64,224]{2,1,0:T(8,128)(2,1)}), bf16[64,64,224]{2,1,0:T(8,128)(2,1)}) %all-gather.14.cloned.1.call-update) | async-done | bytes 1835024 | tf_op jit(solution)/shard_map/all_gather | solution.py:81
  233.4 2.8 gather_fusion.3
  236.2 1.6 broadcast_select_fusion.3
  237.8 1.6 copy.85
  239.4 1.6 copy.87
  241.0 281.5 %all-gather.20.cloned.1.call-done = bf16[16,512,1792]{2,1,0:T(8,128)(2,1)} async-done(((bf16[2,512,1792]{2,1,0:T(8,128)(2,1)}), bf16[16,512,1792]{2,1,0:T(8,128)(2,1)}) %all-gather.20.cloned.1.call-update) | async-done | bytes 29360144 | tf_op jit(solution)/shard_map/all_gather | solution.py:91
  522.5 12.8 %reduce_sum.105 = bf16[2,512,1792]{2,1,0:T(8,128)(2,1)} reduce(bf16[8,2,512,1792]{3,2,1,0:T(8,128)(2,1)} %bitcast.98, bf16[]{:T(256)} %constant.94.clone.1), dimensions={0}, to_apply=%region_3.4 | reduce | flops 12845056 | bytes 33030146 | tf_op jit(solution)/shard_map/reduce_sum | solution.py:91
  535.3 4.5 fusion.4
  539.9 0.9 fusion.6
  540.8 0.9 copy-done.3
  541.7 1.8 copy-done.8
  543.5 2.0 convolution_convert_fusion.3
  545.5 2.1 concatenate.28
  547.6 2.0 copy.88
  549.6 4.2 convolution_convert_fusion.4
  553.8 2.0 convolution_convert_fusion.5
  555.8 2.1 concatenate.25
  558.0 1.8 copy.86
  559.8 2.1 reshape.203
  561.9 2.5 fusion.8
  564.4 1.0 fusion.10
  565.5 1.7 fusion.22
  567.2 3.0 convolution_convert_fusion.1
  570.2 287.4 %all-gather.22.cloned.1.call-done = bf16[16,512,1792]{2,1,0:T(8,128)(2,1)} async-done(((bf16[2,512,1792]{2,1,0:T(8,128)(2,1)}), bf16[16,512,1792]{2,1,0:T(8,128)(2,1)}) %all-gather.22.cloned.1.call-update) | async-done | bytes 29360144 | tf_op jit(solution)/shard_map/all_gather | solution.py:91
  857.6 13.1 %reduce_sum.108 = bf16[2,512,1792]{2,1,0:T(8,128)(2,1)} reduce(bf16[8,2,512,1792]{3,2,1,0:T(8,128)(2,1)} %bitcast.99, bf16[]{:T(256)} %constant.94.clone.1), dimensions={0}, to_apply=%region_7.9 | reduce | flops 12845056 | bytes 33030146 | tf_op jit(solution)/shard_map/reduce_sum | solution.py:91
  870.7 7.4 fusion.9
  878.2 1.3 multiply_convert_fusion
  879.5 1.8 copy-done.10
  881.4 5.8 fusion.68
  887.1 12.5 %convolution_convert_fusion = bf16[1024,1792]{1,0:T(8,128)(2,1)} fusion(bf16[896,1792]{1,0:T(8,128)(2,1)S(1)} %copy-done, f32[1024,896]{1,0:T(8,128)} %fusion.68, bf16[1024,1792]{1,0:T(8,128)(2,1)} %bitcast.107, bf16[1792,896]{1,0:T(8,128)(2,1)} %param.45), kind=kOutput, calls=%fused_computation.26 | convolution fusion | flops 6584008704 | bytes 17432576 | tf_op jit(solution)/shard_map/dot_general | solution.py:184
  900.5 17.6 %pmax.7 = f32[2]{0:T(128)} all-reduce(f32[2]{0:T(128)S(1)} %select_reduce_fusion.1), channel_id=1, replica_groups=mesh['req'=16,'tensor'=8] {'tensor'}, use_global_device_ids=true, to_apply=%region_13.15 | all-reduce | flops 2 | bytes 16 | tf_op jit(solution)/shard_map/pmax | solution.py:196
  918.2 269.2 %all-gather.18.cloned.1.call-done = bf16[8,2,512,1792]{3,2,1,0:T(8,128)(2,1)} async-done(((bf16[1,2,512,1792]{3,2,1,0:T(8,128)(2,1)}), bf16[8,2,512,1792]{3,2,1,0:T(8,128)(2,1)}) %all-gather.18.cloned.1.call-update) | async-done | bytes 29360144 | tf_op jit(solution)/shard_map/all_gather | solution.py:91
  1187.3 12.9 %reduce_sum.110 = bf16[2,512,1792]{2,1,0:T(8,128)(2,1)} reduce(bf16[8,2,512,1792]{3,2,1,0:T(8,128)(2,1)} %all-gather.18.cloned.1.call-done, bf16[]{:T(256)} %constant.94.clone.1), dimensions={0}, to_apply=%region_9.11 | reduce | flops 12845056 | bytes 33030146 | tf_op jit(solution)/shard_map/reduce_sum | solution.py:91
  1200.2 2.2 select_reduce_fusion
  1202.5 16.6 %psum.7 = f32[2]{0:T(128)S(1)} all-reduce(f32[2]{0:T(128)S(1)} %get-tuple-element.4), channel_id=1, replica_groups=mesh['req'=16,'tensor'=8] {'tensor'}, use_global_device_ids=true, to_apply=%region_11.13 | all-reduce | flops 2 | bytes 16 | tf_op jit(solution)/shard_map/psum | solution.py:195
  1219.6 1.9 broadcast_select_fusion.1
  (100 shorter events, 7.1 us)
Async XLA Ops:
  7.2 880.0 %copy-start = (bf16[896,1792]{1,0:T(8,128)(2,1)S(1)}, bf16[896,1792]{1,0:T(8,128)(2,1)}, u32[]{:S(2)}) copy-start(bf16[896,1792]{1,0:T(8,128)(2,1)} %param.46) | copy-start | bytes 9633796
  7.2 58.8 %copy-start.18 = (f32[1792]{0:T(1024)S(1)}, f32[1792]{0:T(1024)}, u32[]{:S(2)}) copy-start(f32[1792]{0:T(1024)} %param.31) | copy-start | bytes 21508
  7.2 55.8 %all-gather.10.cloned.1.call-start = ((), (), s32[]{:S(2)}) async-start(), calls=%async_computation | async-start | bytes 4128768 | tf_op jit(solution)/shard_map/all_gather | solution.py:98
  7.9 129.1 %all-gather.12.cloned.1.call-start = ((), (), s32[]{:S(2)}) async-start(), calls=%async_computation.1 | async-start | bytes 9504768 | tf_op jit(solution)/shard_map/all_gather | solution.py:72
  10.6 174.2 %all-gather.16.cloned.1.call-start = ((), (), s32[]{:S(2)}) async-start(), calls=%async_computation.3 | async-start | bytes 2228224 | tf_op jit(solution)/shard_map/all_gather | solution.py:80
  11.4 222.0 %all-gather.14.cloned.1.call-start = ((), (), s32[]{:S(2)}) async-start(), calls=%async_computation.2 | async-start | bytes 2228224 | tf_op jit(solution)/shard_map/all_gather | solution.py:81
  12.0 510.5 %all-gather.20.cloned.1.call-start = ((), (), s32[]{:S(2)}) async-start(), calls=%async_computation.5 | async-start | bytes 33030144 | tf_op jit(solution)/shard_map/all_gather | solution.py:91
  12.9 2.9 copy-start.28
  63.0 3.1 copy-start.6
  66.1 2.7 copy-start.16
  67.0 1.8 copy-start.1
  77.7 3.5 copy-start.14
  77.7 3.4 copy-start.17
  78.3 1.3 copy-start.7
  81.2 2.1 copy-start.2
  81.2 2.3 copy-start.24
  82.6 2.1 copy-start.21
  82.6 2.1 copy-start.22
  166.6 5.6 copy-start.11
  172.2 3.1 copy-start.29
  175.2 682.4 %all-gather.22.cloned.1.call-start = ((), (), s32[]{:S(2)}) async-start(), calls=%async_computation.6 | async-start | bytes 33030144 | tf_op jit(solution)/shard_map/all_gather | solution.py:91
  535.3 4.6 copy-start.19
  539.9 1.8 copy-start.3
  539.9 3.6 copy-start.25
  541.7 1.8 copy-start.8
  547.6 6.2 copy-start.9
  547.6 6.2 copy-start.26
  564.4 1.0 copy-start.13
  564.4 1.0 copy-start.15
  565.5 1.7 copy-start.12
  570.1 617.2 %all-gather.18.cloned.1.call-start = ((), (), s32[]{:S(2)}) async-start(), calls=%async_computation.4 | async-start | bytes 33030144 | tf_op jit(solution)/shard_map/all_gather | solution.py:91
  870.7 7.4 copy-start.4
  870.7 7.5 copy-start.5
  870.7 7.5 copy-start.20
  878.2 3.2 copy-start.23
  879.5 1.8 copy-start.10
  899.6 0.7 copy-start.27
Sparse Core Ops, SparseCore 0:
  9.6 50.9 all-gather.9
  63.0 73.9 all-gather.11
  139.5 45.2 all-gather.15
  187.1 46.2 all-gather.13
  234.9 287.4 all-gather.19
  570.3 287.3 all-gather.21
  899.8 287.5 all-gather.17
